TPU v7x, 32 devices: a whole 2x2x4 slice. The times are simulated.
32 devices in a mesh: tile: 8 (over y, x, core), chan: 4 (over z).
Axes of the slice: x: 2, y: 2, z: 4, core: 2. Of those that a mesh axis runs over, the one named last changes fastest.
Arguments:
- ensemble: bfloat16 [3072, 128, 256], P('tile', 'chan'), may hold values from -6 to 6
- jacobian: bfloat16 [1280, 128, 128], P('tile', 'chan'), may hold values from -1 to 1
- innovation: float32 [1280, 128], P('tile', 'chan'), may hold values from -6 to 6
- error_vectors: float32 [128, 32], replicated, may hold values from -1 to 1, as said below
- error_values: float32 [128], replicated, may hold values from 0.25 to 4
- ensemble_vectors: float32 [256, 256], replicated, may hold values from -1 to 1, as said below
- column_pick: int32 [8, 5, 40], P('tile'), may hold values from 0 to 383
- footprint_slot: int32 [1280], P('tile'), may hold values from 0 to 199, as said below
- footprint_count: int32 [8], P('tile'), may hold values from 20 to 160, as said below
Outputs:
- analysis: bfloat16 [3072, 128, 256], P('tile', 'chan')
Inputs may be any that keep to these rules, and one draw needn't show every extreme that they name: `footprint_slot`: the 160 entries of one pack are distinct; slot o * 40 + j is the j-th column that tile (pack + 2 - o) mod 8 sends to this pack. `footprint_count`: some pack has all 160 footprints live. `error_vectors`: each block of 32 rows is an orthogonal matrix. `ensemble_vectors`: an orthogonal matrix.
All inputs are finite; a program needn't handle non-finite values.
Results may differ from a plain program's by a relative error of at most 0.013.
Values may be sent and summed in bfloat16 or wider, within the bound.
A program may use at most 64 MiB of HBM per device.

v0:
```python
import jax
import jax.numpy as jnp
from jax import lax
from jax.sharding import PartitionSpec as P


def from_behind(value, axis, steps):
    count = lax.axis_size(axis)
    pairs = [(source, (source + steps) % count) for source in range(count)]
    return lax.ppermute(value, axis, pairs)


def turn_blocks(values, vectors):
    row_count, channels, members = values.shape
    group_width = vectors.shape[1]
    grouped = values.reshape(row_count, channels // group_width, group_width, members)
    basis_blocks = vectors.reshape(channels // group_width, group_width, group_width)
    turned = jnp.einsum("gce,fgck->fgek", basis_blocks, grouped, precision=lax.Precision.HIGHEST)
    return turned.reshape(row_count, channels, members)


def turn_rows(values, vectors):
    row_count, channels = values.shape
    group_width = vectors.shape[1]
    grouped = values.reshape(row_count, channels // group_width, group_width)
    basis_blocks = vectors.reshape(channels // group_width, group_width, group_width)
    turned = jnp.einsum("gce,fgc->fge", basis_blocks, grouped, precision=lax.Precision.HIGHEST)
    return turned.reshape(row_count, channels)


def local(
    ensemble,
    jacobian,
    innovation,
    error_vectors,
    error_values,
    ensemble_vectors,
    column_pick,
    footprint_slot,
    footprint_count,
):
    window = column_pick.shape[1]
    capacity = column_pick.shape[2]
    reach_tiles = window // 2
    level_part = ensemble.shape[1]
    members = ensemble.shape[2]
    chosen = jnp.take(ensemble, column_pick[0].reshape(-1), axis=0).reshape(
        window, capacity, level_part, members
    )
    blocks = []
    for slot_index in range(window):
        shift_by = slot_index - reach_tiles
        if shift_by == 0:
            blocks.append(chosen[slot_index])
        else:
            blocks.append(from_behind(chosen[slot_index], "tile", shift_by))
    arrived = jnp.stack(blocks, 0)
    slot_rows = arrived.reshape(window * capacity, level_part, members)
    columns = jnp.take(slot_rows, footprint_slot, axis=0)
    foot_rows = columns.shape[0]
    live_rows = (jnp.arange(foot_rows, dtype=jnp.int32) < footprint_count[0]).astype(jnp.float32)
    share_rows = foot_rows // lax.axis_size("chan")
    columns, sensitivity, misfit_rows = (
        lax.all_to_all(columns, "chan", split_axis=0, concat_axis=1, tiled=True),
        lax.all_to_all(jacobian, "chan", split_axis=0, concat_axis=1, tiled=True),
        lax.all_to_all(
            innovation.astype(jnp.bfloat16), "chan", split_axis=0, concat_axis=1, tiled=True
        ).astype(innovation.dtype),
    )
    response = jnp.einsum("fcl,flk->fck", sensitivity, columns, preferred_element_type=jnp.float32)
    row_weights = lax.dynamic_slice_in_dim(
        live_rows, lax.axis_index("chan") * share_rows, share_rows, 0
    )
    scales = 1.0 / jnp.sqrt(error_values)
    whitened = (
        turn_blocks(response, error_vectors) * scales[None, :, None] * row_weights[:, None, None]
    )
    misfit = turn_rows(misfit_rows, error_vectors) * scales[None, :]
    pull_sum = jnp.einsum("fck,fc->k", whitened, misfit, precision=lax.Precision.HIGHEST)
    rounded = whitened.astype(jnp.bfloat16).reshape(-1, members)
    gram_sum = lax.dot_general(
        rounded, rounded, (((0,), (0,)), ((), ())), preferred_element_type=jnp.float32
    )
    gram_sum, pull_sum = lax.psum((gram_sum, pull_sum), ("tile", "chan"))
    system = gram_sum + (members - 1) * jnp.eye(members, dtype=jnp.float32)
    factor = jnp.linalg.cholesky(system)
    halfway = lax.linalg.triangular_solve(factor, pull_sum[:, None], left_side=True, lower=True)
    mean_weights = lax.linalg.triangular_solve(
        factor, halfway, left_side=True, lower=True, transpose_a=True
    )[:, 0]
    spread = jnp.sqrt(members - 1.0) * lax.linalg.triangular_solve(
        factor, ensemble_vectors, left_side=True, lower=True, transpose_a=True
    )
    transform = (spread + mean_weights[:, None]).astype(jnp.bfloat16)
    flat_rows = ensemble.reshape(-1, members)
    updated = jnp.dot(flat_rows, transform, preferred_element_type=jnp.float32).astype(jnp.bfloat16)
    return updated.reshape(ensemble.shape)


def solution(mesh):
    return jax.shard_map(
        local,
        mesh=mesh,
        in_specs=(
            P("tile", "chan", None),
            P("tile", "chan", None),
            P("tile", "chan"),
            P(),
            P(),
            P(),
            P("tile", None, None),
            P("tile"),
            P("tile"),
        ),
        out_specs=P("tile", "chan", None),
        check_vma=False,
    )
```

profile of v0, /device:TPU:0, one launch (start us, length us, event | category | flops | bytes accessed | tf_op | source)
XLA Modules:
  0.0 357.7 jit_solution(7432755867193582582)
XLA Ops:
  7.4 5.5 %gather_fusion = bf16[200,32,256]{2,1,0:T(8,128)(2,1)} fusion(bf16[384,32,256]{2,1,0:T(8,128)(2,1)} %param.9, s32[1024]{0:T(1024)S(1)} %pad_clamp_fusion.1), kind=kCustom, calls=%fused_computation | custom fusion | bytes 6554400 | tf_op jit(solution)/shard_map/jit(_take)/gather | solution.py:47
  12.9 2.3 broadcast_select_fusion
  15.3 1.5 fusion.43
  16.8 3.9 %collective-permute-start = (bf16[40,32,256]{2,1,0:T(8,128)(2,1)}, bf16[40,32,256]{2,1,0:T(8,128)(2,1)}, u32[]{:S(2)}, u32[]{:S(2)}) collective-permute-start(bf16[40,32,256]{2,1,0:T(8,128)(2,1)} %get-tuple-element.34), channel_id=1, source_target_pairs={{0,24},{4,28},{8,0},{12,4},{16,8},{20,12},{24,16},{28,20},{1,25},{... | collective-permute-start | bytes 1966088 | tf_op jit(solution)/shard_map/ppermute | solution.py:10
  22.7 4.9 %all-to-all-start.2 = ((bf16[4,2,640]{2,1,0:T(2,128)(2,1)}), bf16[4,2,640]{2,1,0:T(2,128)(2,1)S(1)}, u32[]{:S(2)}, u32[]{:S(2)}) async-start(bf16[4,2,640]{2,1,0:T(2,128)(2,1)} %reshape.193), calls=%async_computation.2 | async-start | bytes 20480 | tf_op jit(solution)/shard_map/all_to_all | solution.py:66
  27.6 5.6 %all-to-all-done.2 = bf16[4,2,640]{2,1,0:T(2,128)(2,1)S(1)} async-done(((bf16[4,2,640]{2,1,0:T(2,128)(2,1)}), bf16[4,2,640]{2,1,0:T(2,128)(2,1)S(1)}, u32[]{:S(2)}, u32[]{:S(2)}) %all-to-all-start.2) | async-done | bytes 10272 | tf_op jit(solution)/shard_map/all_to_all | solution.py:66
  33.2 4.3 %all-to-all-start.1 = ((bf16[160,32,128]{2,1,0:T(8,128)(2,1)}), bf16[160,32,128]{2,1,0:T(8,128)(2,1)}, u32[]{:S(2)}, u32[]{:S(2)}) async-start(bf16[160,32,128]{2,1,0:T(8,128)(2,1)} %param.10), calls=%async_computation.1 | async-start | bytes 2621440 | tf_op jit(solution)/shard_map/all_to_all | solution.py:65
  37.5 1.1 bitcast_dynamic-update-slice_fusion.4
  38.7 11.5 %collective-permute-done.1 = bf16[40,32,256]{2,1,0:T(8,128)(2,1)} collective-permute-done((bf16[40,32,256]{2,1,0:T(8,128)(2,1)}, bf16[40,32,256]{2,1,0:T(8,128)(2,1)}, u32[]{:S(2)}, u32[]{:S(2)}) %collective-permute-start.1) | collective-permute-done | bytes 655392 | tf_op jit(solution)/shard_map/ppermute | solution.py:10
  51.4 1.1 bitcast_dynamic-update-slice_fusion.2
  52.5 11.6 %collective-permute-done.3 = bf16[40,32,256]{2,1,0:T(8,128)(2,1)} collective-permute-done((bf16[40,32,256]{2,1,0:T(8,128)(2,1)}, bf16[40,32,256]{2,1,0:T(8,128)(2,1)}, u32[]{:S(2)}, u32[]{:S(2)}) %collective-permute-start.3) | collective-permute-done | bytes 655392 | tf_op jit(solution)/shard_map/ppermute | solution.py:10
  65.3 1.7 copy-done.1
  67.0 2.7 gather_fusion.1
  69.7 1.8 broadcast_select_fusion.1
  71.5 5.0 %all-to-all-start = ((bf16[160,32,256]{2,1,0:T(8,128)(2,1)}), bf16[160,32,256]{2,1,0:T(8,128)(2,1)S(1)}, u32[]{:S(2)}, u32[]{:S(2)}) async-start(bf16[160,32,256]{2,1,0:T(8,128)(2,1)} %broadcast_select_fusion.1), calls=%async_computation | async-start | bytes 5242880 | tf_op jit(solution)/shard_map/all_to_all | solution.py:64
  77.9 2.8 copy.24
  80.7 54.4 %all-to-all-done = bf16[160,32,256]{2,1,0:T(8,128)(2,1)S(1)} async-done(((bf16[160,32,256]{2,1,0:T(8,128)(2,1)}), bf16[160,32,256]{2,1,0:T(8,128)(2,1)S(1)}, u32[]{:S(2)}, u32[]{:S(2)}) %all-to-all-start) | async-done | bytes 2621472 | tf_op jit(solution)/shard_map/all_to_all | solution.py:64
  137.3 6.6 %multiply_convert_fusion = (bf16[40,4,32,256]{3,2,0,1:T(8,128)(2,1)S(1)}, f32[40,4,32,256]{3,2,0,1:T(8,128)}) fusion(f32[40]{0:T(128)S(1)} %dynamic_slice.3, f32[4,32]{1,0:T(4,128)S(1)} %mul.53, f32[4,32,32,1]{1,0,2,3:T(4,128)S(1)} %bitcast.144, f32[40,4,32,256]{3,2,1,0:T(8,128)S(1)} %bitcast.138), kind=kOutput, calls=%fused_computation.10 | convolution fusion | flops 507248640 | bytes 13124256 | tf_op jit(solution)/shard_map/gce,fgck->fgek/dot_general | solution.py:18
  143.9 1.9 fusion.9
  145.8 2.9 copy.35
  149.8 2.7 fusion.45
  152.5 37.0 %psum.15 = f32[256]{0:T(256)S(1)} all-reduce(f32[256]{0:T(256)S(1)} %bitcast.148), channel_id=1, replica_groups=mesh['tile'=8,'chan'=4] {'tile','chan'}, use_global_device_ids=true, to_apply=%region_5.6 | all-reduce | flops 256 | bytes 2048 | tf_op jit(solution)/shard_map/psum | solution.py:84
  189.5 81.2 %all-reduce.3.cloned.1.call-done = f32[256,256]{0,1:T(8,128)} async-done(((f32[256,256]{0,1:T(8,128)}), f32[256,256]{0,1:T(8,128)}) %all-reduce.3.cloned.1.call-update) | async-done | bytes 262160 | tf_op jit(solution)/shard_map/psum | solution.py:84
  272.8 11.7 %cholesky.49 = f32[128,128]{1,0:T(8,128)S(1)} custom-call(f32[128,128]{1,0:T(8,128)S(1)} %cholesky.115), custom_call_target="Cholesky" | custom-call | tf_op jit(solution)/shard_map/jit(cholesky)/cholesky | solution.py:86
  284.5 9.8 %custom-call.18 = f32[1,128,128]{1,2,0:T(8,128)S(1)} custom-call(f32[1,128,128]{2,1,0:T(8,128)S(1)} %get-tuple-element.36), custom_call_target="InvertDiagBlocksLowerTriangular" | custom-call | tf_op jit(solution)/shard_map/jit(cholesky)/cholesky | solution.py:86
  294.8 11.7 %cholesky.103 = f32[128,128]{1,0:T(8,128)S(1)} custom-call(f32[128,128]{1,0:T(8,128)S(1)} %convolution_subtract_fusion.1), custom_call_target="Cholesky" | custom-call | tf_op jit(solution)/shard_map/jit(cholesky)/cholesky | solution.py:86
  308.9 4.0 %while.1 = (s32[]{:T(128)}, f32[256,256]{0,1:T(8,128)S(1)}, s32[2,2]{1,0:T(2,128)S(1)}, f32[2,128,128]{2,1,0:T(8,128)S(1)}, s32[]{:T(128)}) while((s32[]{:T(128)}, f32[256,256]{0,1:T(8,128)S(1)}, s32[2,2]{1,0:T(2,128)S(1)}, f32[2,128,128]{2,1,0:T(8,128)S(1)}, s32[]{:T(128)}) %tuple.27), condition=%wide.while_cond, body=%wide.while_body.sunk | while | flops 2 | bytes 393321 | solution.py:91
  309.5 1.3 dynamic-slice.7
  311.5 1.3 dynamic-slice.7
  312.9 19.9 %custom-call.19 = f32[2,128,128]{1,2,0:T(8,128)S(1)} custom-call(f32[2,128,128]{2,1,0:T(8,128)S(1)} %get-tuple-element.12), custom_call_target="InvertDiagBlocksLowerTriangular" | custom-call | tf_op jit(solution)/shard_map/triangular_solve | solution.py:91
  334.9 7.4 %fusion = bf16[12288,256]{0,1:T(8,128)(2,1)} fusion(bf16[12288,256]{1,0:T(8,128)(2,1)} %bitcast.139, f32[128,256]{1,0:T(8,128)S(1)} %fusion.23, f32[128,256]{1,0:T(8,128)S(1)} %fusion.32, f32[256]{0:T(256)S(1)} %bitcast.147), kind=kOutput, calls=%fused_computation.5 | convolution fusion | flops 1614020608 | bytes 12846080 | tf_op jit(solution)/shard_map/dot_general | solution.py:96
  342.3 8.6 %copy.38 = bf16[12288,256]{1,0:T(8,128)(2,1)} copy(bf16[12288,256]{0,1:T(8,128)(2,1)} %fusion) | data formatting | bytes 12582912 | tf_op jit(solution)/shard_map/convert_element_type | solution.py:96
  (86 shorter events, 16.1 us)
Async XLA Ops:
  15.2 6.7 %copy-start.3 = (f32[160,32]{0,1:T(8,128)S(1)}, f32[160,32]{0,1:T(8,128)}, u32[]{:S(2)}) copy-start(f32[160,32]{0,1:T(8,128)} %param.11) | copy-start | bytes 61444
  15.3 12.4 %copy-start.5 = (s32[160]{0:T(256)S(1)}, s32[160]{0:T(256)}, u32[]{:S(2)}) copy-start(s32[160]{0:T(256)} %param.16) | copy-start | bytes 1924
  16.8 20.7 %collective-permute-start = (bf16[40,32,256]{2,1,0:T(8,128)(2,1)}, bf16[40,32,256]{2,1,0:T(8,128)(2,1)}, u32[]{:S(2)}, u32[]{:S(2)}) collective-permute-start(bf16[40,32,256]{2,1,0:T(8,128)(2,1)} %get-tuple-element.34), channel_id=1, source_target_pairs={{0,24},{4,28},{8,0},{12,4},{16,8},{20,12},{24,16},{28,20},{1,25},{... | collective-permute-start | bytes 1966088 | tf_op jit(solution)/shard_map/ppermute | solution.py:10
  20.7 29.5 %collective-permute-start.1 = (bf16[40,32,256]{2,1,0:T(8,128)(2,1)}, bf16[40,32,256]{2,1,0:T(8,128)(2,1)}, u32[]{:S(2)}, u32[]{:S(2)}) collective-permute-start(bf16[40,32,256]{2,1,0:T(8,128)(2,1)} %get-tuple-element.33), channel_id=1, source_target_pairs={{0,28},{4,0},{8,4},{12,8},{16,12},{20,16},{24,20},{28,24},{1,29},{... | collective-permute-start | bytes 1966088 | tf_op jit(solution)/shard_map/ppermute | solution.py:10
  20.7 30.7 %collective-permute-start.2 = (bf16[40,32,256]{2,1,0:T(8,128)(2,1)}, bf16[40,32,256]{2,1,0:T(8,128)(2,1)}, u32[]{:S(2)}, u32[]{:S(2)}) collective-permute-start(bf16[40,32,256]{2,1,0:T(8,128)(2,1)} %get-tuple-element.32), channel_id=1, source_target_pairs={{0,4},{4,8},{8,12},{12,16},{16,20},{20,24},{24,28},{28,0},{1,5},{5... | collective-permute-start | bytes 1966088 | tf_op jit(solution)/shard_map/ppermute | solution.py:10
  21.2 42.9 %collective-permute-start.3 = (bf16[40,32,256]{2,1,0:T(8,128)(2,1)}, bf16[40,32,256]{2,1,0:T(8,128)(2,1)}, u32[]{:S(2)}, u32[]{:S(2)}) collective-permute-start(bf16[40,32,256]{2,1,0:T(8,128)(2,1)} %get-tuple-element.31), channel_id=1, source_target_pairs={{0,8},{4,12},{8,16},{12,20},{16,24},{20,28},{24,0},{28,4},{1,9},{5... | collective-permute-start | bytes 1966088 | tf_op jit(solution)/shard_map/ppermute | solution.py:10
  22.7 10.5 %all-to-all-start.2 = ((bf16[4,2,640]{2,1,0:T(2,128)(2,1)}), bf16[4,2,640]{2,1,0:T(2,128)(2,1)S(1)}, u32[]{:S(2)}, u32[]{:S(2)}) async-start(bf16[4,2,640]{2,1,0:T(2,128)(2,1)} %reshape.193), calls=%async_computation.2 | async-start | bytes 20480 | tf_op jit(solution)/shard_map/all_to_all | solution.py:66
  33.2 38.3 %all-to-all-start.1 = ((bf16[160,32,128]{2,1,0:T(8,128)(2,1)}), bf16[160,32,128]{2,1,0:T(8,128)(2,1)}, u32[]{:S(2)}, u32[]{:S(2)}) async-start(bf16[160,32,128]{2,1,0:T(8,128)(2,1)} %param.10), calls=%async_computation.1 | async-start | bytes 2621440 | tf_op jit(solution)/shard_map/all_to_all | solution.py:65
  65.2 1.7 copy-start.1
  71.5 5.7 %copy-start.6 = (f32[128]{0:T(128)S(1)}, f32[128]{0:T(128)}, u32[]{:S(2)}) copy-start(f32[128]{0:T(128)} %param.13) | copy-start | bytes 1540
  71.5 5.8 %copy-start.4 = (f32[128,32]{0,1:T(8,128)S(1)}, f32[128,32]{0,1:T(8,128)}, u32[]{:S(2)}) copy-start(f32[128,32]{0,1:T(8,128)} %param.12) | copy-start | bytes 49156
  71.5 63.6 %all-to-all-start = ((bf16[160,32,256]{2,1,0:T(8,128)(2,1)}), bf16[160,32,256]{2,1,0:T(8,128)(2,1)S(1)}, u32[]{:S(2)}, u32[]{:S(2)}) async-start(bf16[160,32,256]{2,1,0:T(8,128)(2,1)} %broadcast_select_fusion.1), calls=%async_computation | async-start | bytes 5242880 | tf_op jit(solution)/shard_map/all_to_all | solution.py:64
  76.5 194.1 %all-reduce.3.cloned.1.call-start = ((), (), s32[]{:S(2)}) async-start(), calls=%async_computation.3 | async-start | bytes 524288 | tf_op jit(solution)/shard_map/psum | solution.py:84
  135.1 1.3 copy-start
  189.5 144.6 %copy-start.2 = (f32[256,256]{1,0:T(8,128)S(1)}, f32[256,256]{1,0:T(8,128)}, u32[]{:S(2)}) copy-start(f32[256,256]{1,0:T(8,128)} %param.14) | copy-start | bytes 786436
Sparse Core Ops, SparseCore 0:
  145.9 124.6 all-reduce.2
where the time goes:
time: 359 us; the launch traced here: 358 us
  waiting for transfers between devices  164 us (46%)
  other arithmetic  61.9 us (17%)
  local copies, waits for them, and re-layouts  37.6 us (10%)
  blocking collectives  37 us (10%)
  matrix products  21.9 us (6%)
  starting transfers between devices  19.3 us (5%)
  between operations  15.6 us (4%)
    psum x1, waiting for transfers between devices, local(): gram_sum, pull_sum = lax.psum((gram_sum, pull_sum), ('tile', 'chan'))  81.2 us
    all_to_all x1, waiting for transfers between devices, local(): lax.all_to_all(columns, 'chan', split_axis=0, concat_axis=1, tiled=True)  54.4 us
    psum x1, blocking collectives, local(): gram_sum, pull_sum = lax.psum((gram_sum, pull_sum), ('tile', 'chan'))  37 us
    another operation x6, other arithmetic, local(): factor = jnp.linalg.cholesky(system)  33.9 us
    ppermute x4, waiting for transfers between devices, from_behind(): return lax.ppermute(value, axis, pairs)  23.1 us
    another operation x3, other arithmetic, local(): lax.linalg.triangular_solve(factor, ensemble_vectors, left_side=True, low...  20 us
    convert_element_type x1, local copies, waits for them, and re-layouts, local(): jnp.dot(flat_rows, transform, preferred_element_type=jnp.float32)  8.6 us
    dot_general x1, matrix products, local(): jnp.dot(flat_rows, transform, preferred_element_type=jnp.float32)  7.38 us
  transfers between devices with their start and end apart: 8, of which 5 were waited for; matrix products, arithmetic and copies ran while one was open for 6% of the time, Pallas kernels for 0%

commit v1 on v0

--- a/solution.py
+++ b/solution.py
@@ -61,7 +61,12 @@
     live_rows = (jnp.arange(foot_rows, dtype=jnp.int32) < footprint_count[0]).astype(jnp.float32)
     share_rows = foot_rows // lax.axis_size("chan")
     columns, sensitivity, misfit_rows = (
-        lax.all_to_all(columns, "chan", split_axis=0, concat_axis=1, tiled=True),
+        jnp.concatenate(
+            lax.all_to_all(
+                jnp.stack(jnp.split(columns, lax.axis_size("chan"), axis=0)), "chan", 0, 0
+            ),
+            axis=1,
+        ),
         lax.all_to_all(jacobian, "chan", split_axis=0, concat_axis=1, tiled=True),
         lax.all_to_all(
             innovation.astype(jnp.bfloat16), "chan", split_axis=0, concat_axis=1, tiled=True

time: 359 us -> 363 us (1.011)
  transfers between devices with their start and end apart: 8 -> 8, of which waited for: 5 -> 5; matrix products, arithmetic and copies ran while one was open for 6% -> 5% of each run, Pallas kernels for 0% -> 0%
where the time goes in v1:
time: 363 us; the launch traced here: 362 us
  waiting for transfers between devices  167 us (46%)
  other arithmetic  65 us (18%)
  blocking collectives  37 us (10%)
  local copies, waits for them, and re-layouts  35.7 us (10%)
  matrix products  22.5 us (6%)
  starting transfers between devices  19.3 us (5%)
  between operations  15.8 us (4%)
    psum x1, waiting for transfers between devices, local(): gram_sum, pull_sum = lax.psum((gram_sum, pull_sum), ('tile', 'chan'))  83.5 us
    all_to_all x1, waiting for transfers between devices, local(): lax.all_to_all(jnp.stack(jnp.split(columns, lax.axis_size('chan'), axis=0...  54.4 us
    psum x1, blocking collectives, local(): gram_sum, pull_sum = lax.psum((gram_sum, pull_sum), ('tile', 'chan'))  37 us
    another operation x6, other arithmetic, local(): factor = jnp.linalg.cholesky(system)  34 us
    ppermute x4, waiting for transfers between devices, from_behind(): return lax.ppermute(value, axis, pairs)  23.1 us
    another operation x3, other arithmetic, local(): lax.linalg.triangular_solve(factor, ensemble_vectors, left_side=True, low...  20 us
    convert_element_type x1, local copies, waits for them, and re-layouts, local(): jnp.dot(flat_rows, transform, preferred_element_type=jnp.float32)  8.6 us
    dot_general x1, matrix products, local(): jnp.dot(flat_rows, transform, preferred_element_type=jnp.float32)  7.4 us
  transfers between devices with their start and end apart: 8, of which 5 were waited for; matrix products, arithmetic and copies ran while one was open for 5% of the time, Pallas kernels for 0%

profile of v1, /device:TPU:0, one launch (start us, length us, event | category | flops | bytes accessed | tf_op | source)
XLA Modules:
  0.0 361.9 jit_solution(5013113790042947343)
XLA Ops:
  7.4 5.5 %gather_fusion = bf16[200,32,256]{2,1,0:T(8,128)(2,1)} fusion(bf16[384,32,256]{2,1,0:T(8,128)(2,1)} %param.9, s32[1024]{0:T(1024)S(1)} %pad_clamp_fusion.1), kind=kCustom, calls=%fused_computation | custom fusion | bytes 6554400 | tf_op jit(solution)/shard_map/jit(_take)/gather | solution.py:47
  12.9 2.3 broadcast_select_fusion
  15.3 1.5 fusion.43
  16.8 3.9 %collective-permute-start = (bf16[40,32,256]{2,1,0:T(8,128)(2,1)}, bf16[40,32,256]{2,1,0:T(8,128)(2,1)}, u32[]{:S(2)}, u32[]{:S(2)}) collective-permute-start(bf16[40,32,256]{2,1,0:T(8,128)(2,1)} %get-tuple-element.38), channel_id=1, source_target_pairs={{0,24},{4,28},{8,0},{12,4},{16,8},{20,12},{24,16},{28,20},{1,25},{... | collective-permute-start | bytes 1966088 | tf_op jit(solution)/shard_map/ppermute | solution.py:10
  22.7 4.9 %all-to-all-start.2 = ((bf16[4,2,640]{2,1,0:T(2,128)(2,1)}), bf16[4,2,640]{2,1,0:T(2,128)(2,1)S(1)}, u32[]{:S(2)}, u32[]{:S(2)}) async-start(bf16[4,2,640]{2,1,0:T(2,128)(2,1)} %reshape.201), calls=%async_computation.2 | async-start | bytes 20480 | tf_op jit(solution)/shard_map/all_to_all | solution.py:71
  27.6 5.6 %all-to-all-done.2 = bf16[4,2,640]{2,1,0:T(2,128)(2,1)S(1)} async-done(((bf16[4,2,640]{2,1,0:T(2,128)(2,1)}), bf16[4,2,640]{2,1,0:T(2,128)(2,1)S(1)}, u32[]{:S(2)}, u32[]{:S(2)}) %all-to-all-start.2) | async-done | bytes 10272 | tf_op jit(solution)/shard_map/all_to_all | solution.py:71
  33.2 4.3 %all-to-all-start.1 = ((bf16[160,32,128]{2,1,0:T(8,128)(2,1)}), bf16[160,32,128]{2,1,0:T(8,128)(2,1)}, u32[]{:S(2)}, u32[]{:S(2)}) async-start(bf16[160,32,128]{2,1,0:T(8,128)(2,1)} %param.10), calls=%async_computation.1 | async-start | bytes 2621440 | tf_op jit(solution)/shard_map/all_to_all | solution.py:70
  37.5 1.1 bitcast_dynamic-update-slice_fusion.4
  38.7 11.5 %collective-permute-done.1 = bf16[40,32,256]{2,1,0:T(8,128)(2,1)} collective-permute-done((bf16[40,32,256]{2,1,0:T(8,128)(2,1)}, bf16[40,32,256]{2,1,0:T(8,128)(2,1)}, u32[]{:S(2)}, u32[]{:S(2)}) %collective-permute-start.1) | collective-permute-done | bytes 655392 | tf_op jit(solution)/shard_map/ppermute | solution.py:10
  51.4 1.1 bitcast_dynamic-update-slice_fusion.2
  52.5 11.6 %collective-permute-done.3 = bf16[40,32,256]{2,1,0:T(8,128)(2,1)} collective-permute-done((bf16[40,32,256]{2,1,0:T(8,128)(2,1)}, bf16[40,32,256]{2,1,0:T(8,128)(2,1)}, u32[]{:S(2)}, u32[]{:S(2)}) %collective-permute-start.3) | collective-permute-done | bytes 655392 | tf_op jit(solution)/shard_map/ppermute | solution.py:10
  65.3 1.7 copy-done.1
  67.0 2.7 gather_fusion.1
  70.3 1.8 pad_maximum_fusion
  72.1 5.0 %all-to-all-start = ((bf16[4,40,32,256]{3,2,1,0:T(8,128)(2,1)}), bf16[4,40,32,256]{3,2,1,0:T(8,128)(2,1)S(1)}, u32[]{:S(2)}, u32[]{:S(2)}) async-start(bf16[4,40,32,256]{3,2,1,0:T(8,128)(2,1)} %pad_maximum_fusion), calls=%async_computation | async-start | bytes 5242880 | tf_op jit(solution)/shard_map/all_to_all | solution.py:65
  78.5 2.8 copy.45
  81.3 54.4 %all-to-all-done = bf16[4,40,32,256]{3,2,1,0:T(8,128)(2,1)S(1)} async-done(((bf16[4,40,32,256]{3,2,1,0:T(8,128)(2,1)}), bf16[4,40,32,256]{3,2,1,0:T(8,128)(2,1)S(1)}, u32[]{:S(2)}, u32[]{:S(2)}) %all-to-all-start) | async-done | bytes 2621472 | tf_op jit(solution)/shard_map/all_to_all | solution.py:65
  137.9 5.5 %multiply_convert_fusion = (bf16[40,4,32,256]{3,2,0,1:T(8,128)(2,1)S(1)}, f32[40,4,32,256]{3,2,0,1:T(8,128)S(1)}) fusion(f32[40]{0:T(128)S(1)} %dynamic_slice.3, f32[4,32]{1,0:T(4,128)S(1)} %mul.53, f32[4,32,32,1]{1,0,2,3:T(4,128)S(1)} %bitcast.150, f32[40,4,32,256]{3,2,1,0:T(8,128)S(1)} %bitcast.144), kind=kOutput, calls=%fused_computation.10 | convolution fusion | flops 507248640 | bytes 13124256 | tf_op jit(solution)/shard_map/gce,fgck->fgek/dot_general | solution.py:18
  143.8 3.7 %fusion.1 = f32[40,128,256]{2,1,0:T(8,128)} fusion(f32[40,4,32,256]{3,2,1,0:T(8,128)S(1)} %copy.56, f32[40]{0:T(128)S(1)} %dynamic_slice.3, f32[128]{0:T(128)S(1)} %sqrt.3), kind=kLoop, calls=%fused_computation.7 | loop fusion | flops 2621440 | bytes 10486432 | tf_op jit(solution)/shard_map/mul | solution.py:81
  147.5 1.9 fusion.9
  149.5 4.4 %fusion.45 = f32[1,256,1]{1,0,2:T(1,128)S(1)} fusion(f32[40,128,256]{2,1,0:T(8,128)} %fusion.1, f32[40,128,1]{1,2,0:T(1,128)S(1)} %copy.62), kind=kOutput, calls=%fused_computation.95 | convolution fusion | flops 15728640 | bytes 5264384 | tf_op jit(solution)/shard_map/fck,fc->k/dot_general | solution.py:84
  153.8 37.0 %psum.15 = f32[256]{0:T(256)S(1)} all-reduce(f32[256]{0:T(256)S(1)} %bitcast.154), channel_id=1, replica_groups=mesh['tile'=8,'chan'=4] {'tile','chan'}, use_global_device_ids=true, to_apply=%region_5.6 | all-reduce | flops 256 | bytes 2048 | tf_op jit(solution)/shard_map/psum | solution.py:89
  190.9 83.5 %all-reduce.3.cloned.1.call-done = f32[256,256]{0,1:T(8,128)} async-done(((f32[256,256]{0,1:T(8,128)}), f32[256,256]{0,1:T(8,128)}) %all-reduce.3.cloned.1.call-update) | async-done | bytes 262160 | tf_op jit(solution)/shard_map/psum | solution.py:89
  276.5 11.7 %cholesky.49 = f32[128,128]{1,0:T(8,128)S(1)} custom-call(f32[128,128]{1,0:T(8,128)S(1)} %cholesky.115), custom_call_target="Cholesky" | custom-call | tf_op jit(solution)/shard_map/jit(cholesky)/cholesky | solution.py:91
  288.2 9.8 %custom-call.18 = f32[1,128,128]{1,2,0:T(8,128)S(1)} custom-call(f32[1,128,128]{2,1,0:T(8,128)S(1)} %get-tuple-element.44), custom_call_target="InvertDiagBlocksLowerTriangular" | custom-call | tf_op jit(solution)/shard_map/jit(cholesky)/cholesky | solution.py:91
  298.5 11.7 %cholesky.103 = f32[128,128]{1,0:T(8,128)S(1)} custom-call(f32[128,128]{1,0:T(8,128)S(1)} %convolution_subtract_fusion.1), custom_call_target="Cholesky" | custom-call | tf_op jit(solution)/shard_map/jit(cholesky)/cholesky | solution.py:91
  312.8 4.3 %while.1 = (s32[]{:T(128)}, f32[256,256]{0,1:T(8,128)S(1)}, s32[2,2]{1,0:T(2,128)S(1)}, f32[2,128,128]{2,1,0:T(8,128)S(1)}, s32[]{:T(128)}) while((s32[]{:T(128)}, f32[256,256]{0,1:T(8,128)S(1)}, s32[2,2]{1,0:T(2,128)S(1)}, f32[2,128,128]{2,1,0:T(8,128)S(1)}, s32[]{:T(128)}) %tuple.31), condition=%wide.while_cond, body=%wide.while_body.sunk | while | flops 2 | bytes 393321 | solution.py:96
  313.4 1.4 dynamic-slice.7
  315.6 1.4 dynamic-slice.7
  317.2 19.9 %custom-call.19 = f32[2,128,128]{1,2,0:T(8,128)S(1)} custom-call(f32[2,128,128]{2,1,0:T(8,128)S(1)} %get-tuple-element.12), custom_call_target="InvertDiagBlocksLowerTriangular" | custom-call | tf_op jit(solution)/shard_map/triangular_solve | solution.py:96
  339.1 7.4 %fusion = bf16[12288,256]{0,1:T(8,128)(2,1)} fusion(bf16[12288,256]{1,0:T(8,128)(2,1)} %bitcast.145, f32[128,256]{1,0:T(8,128)S(1)} %fusion.23, f32[128,256]{1,0:T(8,128)S(1)} %fusion.32, f32[256]{0:T(256)S(1)} %bitcast.153), kind=kOutput, calls=%fused_computation.5 | convolution fusion | flops 1614020608 | bytes 12846080 | tf_op jit(solution)/shard_map/dot_general | solution.py:101
  346.5 8.6 %copy.59 = bf16[12288,256]{1,0:T(8,128)(2,1)} copy(bf16[12288,256]{0,1:T(8,128)(2,1)} %fusion) | data formatting | bytes 12582912 | tf_op jit(solution)/shard_map/convert_element_type | solution.py:101
  (88 shorter events, 16.2 us)
Async XLA Ops:
  15.2 6.7 %copy-start.3 = (f32[160,32]{0,1:T(8,128)S(1)}, f32[160,32]{0,1:T(8,128)}, u32[]{:S(2)}) copy-start(f32[160,32]{0,1:T(8,128)} %param.11) | copy-start | bytes 61444
  15.3 12.4 %copy-start.5 = (s32[160]{0:T(256)S(1)}, s32[160]{0:T(256)}, u32[]{:S(2)}) copy-start(s32[160]{0:T(256)} %param.16) | copy-start | bytes 1924
  16.8 20.7 %collective-permute-start = (bf16[40,32,256]{2,1,0:T(8,128)(2,1)}, bf16[40,32,256]{2,1,0:T(8,128)(2,1)}, u32[]{:S(2)}, u32[]{:S(2)}) collective-permute-start(bf16[40,32,256]{2,1,0:T(8,128)(2,1)} %get-tuple-element.38), channel_id=1, source_target_pairs={{0,24},{4,28},{8,0},{12,4},{16,8},{20,12},{24,16},{28,20},{1,25},{... | collective-permute-start | bytes 1966088 | tf_op jit(solution)/shard_map/ppermute | solution.py:10
  20.7 29.5 %collective-permute-start.1 = (bf16[40,32,256]{2,1,0:T(8,128)(2,1)}, bf16[40,32,256]{2,1,0:T(8,128)(2,1)}, u32[]{:S(2)}, u32[]{:S(2)}) collective-permute-start(bf16[40,32,256]{2,1,0:T(8,128)(2,1)} %get-tuple-element.37), channel_id=1, source_target_pairs={{0,28},{4,0},{8,4},{12,8},{16,12},{20,16},{24,20},{28,24},{1,29},{... | collective-permute-start | bytes 1966088 | tf_op jit(solution)/shard_map/ppermute | solution.py:10
  20.7 30.7 %collective-permute-start.2 = (bf16[40,32,256]{2,1,0:T(8,128)(2,1)}, bf16[40,32,256]{2,1,0:T(8,128)(2,1)}, u32[]{:S(2)}, u32[]{:S(2)}) collective-permute-start(bf16[40,32,256]{2,1,0:T(8,128)(2,1)} %get-tuple-element.36), channel_id=1, source_target_pairs={{0,4},{4,8},{8,12},{12,16},{16,20},{20,24},{24,28},{28,0},{1,5},{5... | collective-permute-start | bytes 1966088 | tf_op jit(solution)/shard_map/ppermute | solution.py:10
  21.2 42.9 %collective-permute-start.3 = (bf16[40,32,256]{2,1,0:T(8,128)(2,1)}, bf16[40,32,256]{2,1,0:T(8,128)(2,1)}, u32[]{:S(2)}, u32[]{:S(2)}) collective-permute-start(bf16[40,32,256]{2,1,0:T(8,128)(2,1)} %get-tuple-element.35), channel_id=1, source_target_pairs={{0,8},{4,12},{8,16},{12,20},{16,24},{20,28},{24,0},{28,4},{1,9},{5... | collective-permute-start | bytes 1966088 | tf_op jit(solution)/shard_map/ppermute | solution.py:10
  22.7 10.5 %all-to-all-start.2 = ((bf16[4,2,640]{2,1,0:T(2,128)(2,1)}), bf16[4,2,640]{2,1,0:T(2,128)(2,1)S(1)}, u32[]{:S(2)}, u32[]{:S(2)}) async-start(bf16[4,2,640]{2,1,0:T(2,128)(2,1)} %reshape.201), calls=%async_computation.2 | async-start | bytes 20480 | tf_op jit(solution)/shard_map/all_to_all | solution.py:71
  33.2 38.9 %all-to-all-start.1 = ((bf16[160,32,128]{2,1,0:T(8,128)(2,1)}), bf16[160,32,128]{2,1,0:T(8,128)(2,1)}, u32[]{:S(2)}, u32[]{:S(2)}) async-start(bf16[160,32,128]{2,1,0:T(8,128)(2,1)} %param.10), calls=%async_computation.1 | async-start | bytes 2621440 | tf_op jit(solution)/shard_map/all_to_all | solution.py:70
  65.2 1.7 copy-start.1
  72.1 5.7 %copy-start.6 = (f32[128]{0:T(128)S(1)}, f32[128]{0:T(128)}, u32[]{:S(2)}) copy-start(f32[128]{0:T(128)} %param.13) | copy-start | bytes 1540
  72.1 5.8 %copy-start.4 = (f32[128,32]{0,1:T(8,128)S(1)}, f32[128,32]{0,1:T(8,128)}, u32[]{:S(2)}) copy-start(f32[128,32]{0,1:T(8,128)} %param.12) | copy-start | bytes 49156
  72.1 63.6 %all-to-all-start = ((bf16[4,40,32,256]{3,2,1,0:T(8,128)(2,1)}), bf16[4,40,32,256]{3,2,1,0:T(8,128)(2,1)S(1)}, u32[]{:S(2)}, u32[]{:S(2)}) async-start(bf16[4,40,32,256]{3,2,1,0:T(8,128)(2,1)} %pad_maximum_fusion), calls=%async_computation | async-start | bytes 5242880 | tf_op jit(solution)/shard_map/all_to_all | solution.py:65
  77.2 197.2 %all-reduce.3.cloned.1.call-start = ((), (), s32[]{:S(2)}) async-start(), calls=%async_computation.3 | async-start | bytes 524288 | tf_op jit(solution)/shard_map/psum | solution.py:89
  135.7 1.3 copy-start
  190.9 147.4 %copy-start.2 = (f32[256,256]{1,0:T(8,128)S(1)}, f32[256,256]{1,0:T(8,128)}, u32[]{:S(2)}) copy-start(f32[256,256]{1,0:T(8,128)} %param.14) | copy-start | bytes 786436
Sparse Core Ops, SparseCore 0:
  149.6 124.7 all-reduce.2
